TPU v7x, 32 devices: a whole 2x2x4 slice. The times are simulated.
32 devices in a mesh: wide: 8 (over z, y), narrow: 4 (over x, core).
Axes of the slice: x: 2, y: 2, z: 4, core: 2. Of those that a mesh axis runs over, the one named last changes fastest.
Arguments:
- media_feats: bfloat16 [8, 2048, 1536], P('wide', 'narrow'), may hold values from -6 to 6
- latents: bfloat16 [8, 64, 1536], P('wide', 'narrow'), may hold values from -6 to 6
- frame_counts: int32 [8], P('wide'), may hold values from 1 to 8, as said below
- media_mask: int32 [8, 2048], P('wide'), may hold values 0 or 1
- time_embed: bfloat16 [8, 1536], replicated, may hold values from -3 to 3
- media_gain: float32 [1536], replicated, may hold values from 0.1 to 1.9
- media_bias: float32 [1536], replicated, may hold values from -1.75 to 1.75
- latent_gain: float32 [1536], replicated, may hold values from 0.1 to 1.9
- latent_bias: float32 [1536], replicated, may hold values from -1.75 to 1.75
- ffn_gain: float32 [1536], replicated, may hold values from 0.1 to 1.9
- ffn_bias: float32 [1536], replicated, may hold values from -1.75 to 1.75
- query_weight: bfloat16 [1536, 1536], P('wide', 'narrow'), may hold values from -0.3125 to 0.3125
- keyval_weight: bfloat16 [1536, 2, 1536], P('wide', None, 'narrow'), may hold values from -0.15625 to 0.15625
- output_weight: bfloat16 [1536, 1536], P('narrow', 'wide'), may hold values from -0.625 to 0.625
- up_weight: bfloat16 [1536, 6144], P(None, 'narrow'), may hold values from -0.15625 to 0.15625
- down_weight: bfloat16 [6144, 1536], P('narrow'), may hold values from -0.078125 to 0.078125
- cotangent: bfloat16 [8, 64, 1536], P('wide', 'narrow'), may hold values from -6 to 6
Outputs:
- out_latents: bfloat16 [8, 64, 1536], P('wide', 'narrow')
- grad_media: bfloat16 [8, 2048, 1536], P('wide', 'narrow')
- grad_latents: bfloat16 [8, 64, 1536], P('wide', 'narrow')
- grad_time_embed: float32 [8, 1536], P(None, ('wide', 'narrow'))
- grad_media_gain: float32 [1536], P(('wide', 'narrow'))
- grad_media_bias: float32 [1536], P(('wide', 'narrow'))
- grad_latent_gain: float32 [1536], P(('wide', 'narrow'))
- grad_latent_bias: float32 [1536], P(('wide', 'narrow'))
- grad_ffn_gain: float32 [1536], P(('wide', 'narrow'))
- grad_ffn_bias: float32 [1536], P(('wide', 'narrow'))
- grad_query_weight: float32 [1536, 1536], P('wide', 'narrow')
- grad_keyval_weight: float32 [1536, 2, 1536], P('wide', None, 'narrow')
- grad_output_weight: float32 [1536, 1536], P('narrow', 'wide')
- grad_up_weight: float32 [1536, 6144], P('wide', 'narrow')
- grad_down_weight: float32 [6144, 1536], P('narrow', 'wide')
Inputs may be any that keep to these rules, and one draw needn't show every extreme that they name: `frame_counts`: frames of each item; some item has exactly 8.
All inputs are finite; a program needn't handle non-finite values. No bound on the sum of `media_mask` on one device may be relied on, other than what follows from the above.
Results may differ from a plain program's by a relative error of at most 0.02.
Values may be sent and summed in bfloat16 or wider, within the bound.
A program may use at most 128 MiB of HBM per device.

v0:
```python
import math
import jax
import jax.numpy as jnp
from jax import lax
from jax.sharding import PartitionSpec as P

HEADS = 16
HEAD_DIM = 96
FRAMES_MAX = 8
PATCHES = 256
EPS = 1e-05
ENT_COEF = 4.0
HIGH = lax.Precision.HIGHEST


def norm_forward(values, norm_gain, norm_bias):
    row_mean = jnp.mean(values, axis=-1, keepdims=True)
    centered = values - row_mean
    inv_std = lax.rsqrt(jnp.mean(centered * centered, axis=-1, keepdims=True) + EPS)
    normed = centered * inv_std
    return (normed * norm_gain + norm_bias, normed, inv_std)


def norm_backward(grad_out, normed, inv_std, norm_gain):
    scaled = grad_out * norm_gain
    grad_in = inv_std * (
        scaled
        - jnp.mean(scaled, axis=-1, keepdims=True)
        - normed * jnp.mean(scaled * normed, axis=-1, keepdims=True)
    )
    return (grad_in, jnp.sum(grad_out * normed, axis=0), jnp.sum(grad_out, axis=0))


def gelu_slope(pre_act):
    cdf_part = 0.5 * (1.0 + lax.erf(pre_act * (1.0 / math.sqrt(2.0))))
    density = jnp.exp(-0.5 * pre_act * pre_act) * (1.0 / math.sqrt(2.0 * math.pi))
    return cdf_part + pre_act * density


def body(
    media_feats,
    latents,
    frame_counts,
    media_mask,
    time_embed,
    media_gain,
    media_bias,
    latent_gain,
    latent_bias,
    ffn_gain,
    ffn_bias,
    query_weight,
    keyval_weight,
    output_weight,
    up_weight,
    down_weight,
    cotangent,
):
    item_count = media_feats.shape[0]
    own_media = media_feats.shape[1]
    width = media_feats.shape[2]
    own_latent = latents.shape[1]
    narrow_size = lax.axis_size("narrow")
    narrow_pos = lax.axis_index("narrow")
    media_total = own_media * narrow_size
    latent_total = own_latent * narrow_size
    head_local = HEADS // narrow_size
    cols = head_local * HEAD_DIM
    key_total = media_total + latent_total
    all_ids = jnp.arange(media_total, dtype=jnp.int32) // PATCHES
    valid_tok = (all_ids[None, :] < frame_counts[:, None]) & (media_mask > 0)
    local_count = jnp.sum(valid_tok.astype(jnp.float32)) + float(item_count * latent_total)
    total_count = lax.psum(local_count, "wide")
    all_items = item_count * lax.axis_size("wide")
    ent_weight = ENT_COEF * float(all_items * media_total) / total_count
    query_own, keyval_own, output_own = (
        lax.all_gather(query_weight, "wide", axis=0, tiled=True),
        lax.all_gather(keyval_weight, "wide", axis=0, tiled=True),
        lax.all_gather(output_weight, "wide", axis=1, tiled=True),
    )
    query_full, keyval_full = (
        lax.all_gather(query_own, "narrow", axis=1, tiled=True),
        lax.all_gather(keyval_own, "narrow", axis=2, tiled=True),
    )
    keyval_flat = keyval_own.reshape(width, 2 * cols)
    own_ids = (narrow_pos * own_media + jnp.arange(own_media, dtype=jnp.int32)) // PATCHES
    frame_onehot = own_ids[:, None] == jnp.arange(FRAMES_MAX, dtype=jnp.int32)[None, :]
    time_rows = jnp.dot(
        frame_onehot.astype(jnp.bfloat16), time_embed, preferred_element_type=jnp.float32
    )
    score_scale = HEAD_DIM ** (-0.5)

    def item_step(carry, item):
        (
            down_acc,
            up_acc,
            output_acc,
            keyval_acc,
            query_acc,
            mg_acc,
            mb_acc,
            lg_acc,
            lb_acc,
            fg_acc,
            fb_acc,
            time_acc,
        ) = carry
        media_one, latent_one, valid_one, cot_one = item
        media_nf, media_hat, media_istd = norm_forward(
            media_one.astype(jnp.float32) + time_rows, media_gain, media_bias
        )
        latent_f32 = latent_one.astype(jnp.float32)
        latent_nf, latent_hat, latent_istd = norm_forward(latent_f32, latent_gain, latent_bias)
        media_all, latent_all = (
            lax.all_gather(media_nf.astype(jnp.bfloat16), "narrow", axis=0, tiled=True),
            lax.all_gather(latent_nf.astype(jnp.bfloat16), "narrow", axis=0, tiled=True),
        )
        keys_in = jnp.concatenate([media_all, latent_all], axis=0)
        query_act = jnp.dot(latent_all, query_own, preferred_element_type=jnp.float32).astype(
            jnp.bfloat16
        )
        key_vals = jnp.dot(keys_in, keyval_flat, preferred_element_type=jnp.float32).astype(
            jnp.bfloat16
        )
        query_heads = query_act.reshape(latent_total, head_local, HEAD_DIM)
        key_heads = key_vals[:, :cols].reshape(key_total, head_local, HEAD_DIM)
        value_heads = key_vals[:, cols:].reshape(key_total, head_local, HEAD_DIM)
        key_valid = jnp.concatenate([valid_one, jnp.ones((latent_total,), dtype=bool)])
        scores = (
            jnp.einsum("lhd,khd->hlk", query_heads, key_heads, preferred_element_type=jnp.float32)
            * score_scale
        )
        open_keys = key_valid[None, None, :]
        masked = jnp.where(open_keys, scores, -1e30)
        row_top = jnp.max(masked, axis=-1)
        expo = jnp.exp(masked - row_top[..., None])
        prob_all = expo / jnp.sum(expo, axis=-1)[..., None]
        prob_low = prob_all.astype(jnp.bfloat16)
        plain_scores = jnp.where(open_keys, scores, 0.0)
        mean_score = jnp.sum(prob_all * plain_scores, axis=-1)
        attn_out = jnp.einsum(
            "hlk,khd->lhd", prob_low, value_heads, preferred_element_type=jnp.float32
        ).reshape(latent_total, cols)
        attn_low = attn_out.astype(jnp.bfloat16)
        branch_part = jnp.dot(attn_low, output_own, preferred_element_type=jnp.float32)
        branch_own = lax.psum_scatter(
            branch_part.astype(jnp.bfloat16), "narrow", scatter_dimension=0, tiled=True
        ).astype(jnp.float32)
        latent_mid = latent_f32 + branch_own
        hidden_f, hidden_hat, hidden_istd = norm_forward(latent_mid, ffn_gain, ffn_bias)
        hidden_all, cot_all = (
            lax.all_gather(hidden_f.astype(jnp.bfloat16), "narrow", axis=0, tiled=True),
            lax.all_gather(cot_one, "narrow", axis=0, tiled=True),
        )
        pre_act = jnp.dot(hidden_all, up_weight, preferred_element_type=jnp.float32)
        act_low = jax.nn.gelu(pre_act, approximate=False).astype(jnp.bfloat16)
        ffn_part = jnp.dot(act_low, down_weight, preferred_element_type=jnp.float32)
        ffn_own = lax.psum_scatter(
            ffn_part.astype(jnp.bfloat16), "narrow", scatter_dimension=0, tiled=True
        ).astype(jnp.float32)
        out_one = (latent_mid + ffn_own).astype(jnp.bfloat16)
        down_acc = down_acc + jnp.einsum(
            "lf,ld->fd", act_low, cot_all, preferred_element_type=jnp.float32
        )
        grad_act = jnp.einsum("ld,fd->lf", cot_all, down_weight, preferred_element_type=jnp.float32)
        grad_pre = (grad_act * gelu_slope(pre_act)).astype(jnp.bfloat16)
        up_acc = up_acc + jnp.einsum(
            "ld,lf->df", hidden_all, grad_pre, preferred_element_type=jnp.float32
        )
        hidden_part = jnp.einsum(
            "lf,df->ld", grad_pre, up_weight, preferred_element_type=jnp.float32
        )
        grad_hidden = lax.psum_scatter(
            hidden_part.astype(jnp.bfloat16), "narrow", scatter_dimension=0, tiled=True
        ).astype(jnp.float32)
        grad_norm, fg_part, fb_part = norm_backward(grad_hidden, hidden_hat, hidden_istd, ffn_gain)
        grad_mid = cot_one.astype(jnp.float32) + grad_norm
        grad_branch_all = lax.all_gather(
            grad_mid.astype(jnp.bfloat16), "narrow", axis=0, tiled=True
        )
        output_acc = output_acc + jnp.einsum(
            "lc,ld->cd", attn_low, grad_branch_all, preferred_element_type=jnp.float32
        )
        grad_attn = jnp.einsum(
            "ld,cd->lc", grad_branch_all, output_own, preferred_element_type=jnp.float32
        ).astype(jnp.bfloat16)
        row_dots = jnp.sum(
            (grad_attn.astype(jnp.float32) * attn_out).reshape(latent_total, head_local, HEAD_DIM),
            axis=-1,
        )
        shift_rows = (jnp.transpose(row_dots, (1, 0)) - ent_weight * mean_score)[..., None]
        grad_heads = grad_attn.reshape(latent_total, head_local, HEAD_DIM)
        grad_prob = jnp.einsum(
            "lhd,khd->hlk", grad_heads, value_heads, preferred_element_type=jnp.float32
        )
        grad_scores = (prob_all * (grad_prob - ent_weight * plain_scores - shift_rows)).astype(
            jnp.bfloat16
        )
        grad_values = jnp.einsum(
            "hlk,lhd->khd", prob_low, grad_heads, preferred_element_type=jnp.float32
        ).reshape(key_total, cols)
        grad_keys = (
            jnp.einsum(
                "hlk,lhd->khd", grad_scores, query_heads, preferred_element_type=jnp.float32
            ).reshape(key_total, cols)
            * score_scale
        )
        grad_query = (
            jnp.einsum(
                "hlk,khd->lhd", grad_scores, key_heads, preferred_element_type=jnp.float32
            ).reshape(latent_total, cols)
            * score_scale
        ).astype(jnp.bfloat16)
        grad_pairs = jnp.concatenate([grad_keys, grad_values], axis=-1).astype(jnp.bfloat16)
        keyval_acc = keyval_acc + jnp.einsum(
            "kd,ke->de", keys_in, grad_pairs, preferred_element_type=jnp.float32
        )
        query_acc = query_acc + jnp.einsum(
            "ld,lc->dc", latent_all, grad_query, preferred_element_type=jnp.float32
        )
        media_pairs = grad_pairs[:media_total].reshape(media_total, 2, cols)
        latent_pairs = jnp.concatenate(
            [
                grad_pairs[media_total:].reshape(latent_total, 2, cols),
                grad_query.reshape(latent_total, 1, cols),
            ],
            axis=1,
        )
        media_back, latent_back = (
            lax.all_to_all(media_pairs, "narrow", split_axis=0, concat_axis=2, tiled=True),
            lax.all_to_all(latent_pairs, "narrow", split_axis=0, concat_axis=2, tiled=True),
        )
        grad_media_rows = jnp.einsum(
            "rsc,dsc->rd", media_back, keyval_full, preferred_element_type=jnp.float32
        )
        grad_latent_normed = jnp.einsum(
            "rsc,dsc->rd", latent_back[:, :2], keyval_full, preferred_element_type=jnp.float32
        ) + jnp.einsum(
            "rc,dc->rd", latent_back[:, 2], query_full, preferred_element_type=jnp.float32
        )
        grad_media_in, mg_part, mb_part = norm_backward(
            grad_media_rows, media_hat, media_istd, media_gain
        )
        time_acc = time_acc + jnp.einsum(
            "mf,md->fd", frame_onehot.astype(jnp.float32), grad_media_in, precision=HIGH
        )
        grad_latent_in, lg_part, lb_part = norm_backward(
            grad_latent_normed, latent_hat, latent_istd, latent_gain
        )
        grad_latent_one = (grad_mid + grad_latent_in).astype(jnp.bfloat16)
        carry = (
            down_acc,
            up_acc,
            output_acc,
            keyval_acc,
            query_acc,
            mg_acc + mg_part,
            mb_acc + mb_part,
            lg_acc + lg_part,
            lb_acc + lb_part,
            fg_acc + fg_part,
            fb_acc + fb_part,
            time_acc,
        )
        return (carry, (out_one, grad_media_in.astype(jnp.bfloat16), grad_latent_one))

    ff_local = up_weight.shape[1]
    vector_zero = jnp.zeros((width,), jnp.float32)
    start = (
        jnp.zeros((ff_local, width), jnp.float32),
        jnp.zeros((width, ff_local), jnp.float32),
        jnp.zeros((cols, width), jnp.float32),
        jnp.zeros((width, 2 * cols), jnp.float32),
        jnp.zeros((width, cols), jnp.float32),
        vector_zero,
        vector_zero,
        vector_zero,
        vector_zero,
        vector_zero,
        vector_zero,
        jnp.zeros((FRAMES_MAX, width), jnp.float32),
    )
    totals, stacked = lax.scan(item_step, start, (media_feats, latents, valid_tok, cotangent))
    (
        down_acc,
        up_acc,
        output_acc,
        keyval_acc,
        query_acc,
        mg_acc,
        mb_acc,
        lg_acc,
        lb_acc,
        fg_acc,
        fb_acc,
        time_acc,
    ) = totals
    out_latents, grad_media, grad_latents = stacked
    up_sum, down_sum, query_sum, keyval_sum, output_sum = (
        lax.psum_scatter(
            up_acc.astype(jnp.bfloat16), "wide", scatter_dimension=0, tiled=True
        ).astype(jnp.float32),
        lax.psum_scatter(
            down_acc.astype(jnp.bfloat16), "wide", scatter_dimension=1, tiled=True
        ).astype(jnp.float32),
        lax.psum_scatter(
            query_acc.astype(jnp.bfloat16), "wide", scatter_dimension=0, tiled=True
        ).astype(jnp.float32),
        lax.psum_scatter(
            keyval_acc.reshape(width, 2, cols).astype(jnp.bfloat16),
            "wide",
            scatter_dimension=0,
            tiled=True,
        ).astype(jnp.float32),
        lax.psum_scatter(
            output_acc.astype(jnp.bfloat16), "wide", scatter_dimension=1, tiled=True
        ).astype(jnp.float32),
    )
    mg_sum, mb_sum, lg_sum, lb_sum, fg_sum, fb_sum, time_sum = (
        lax.psum_scatter(mg_acc, ("wide", "narrow"), scatter_dimension=0, tiled=True),
        lax.psum_scatter(mb_acc, ("wide", "narrow"), scatter_dimension=0, tiled=True),
        lax.psum_scatter(lg_acc, ("wide", "narrow"), scatter_dimension=0, tiled=True),
        lax.psum_scatter(lb_acc, ("wide", "narrow"), scatter_dimension=0, tiled=True),
        lax.psum_scatter(fg_acc, ("wide", "narrow"), scatter_dimension=0, tiled=True),
        lax.psum_scatter(fb_acc, ("wide", "narrow"), scatter_dimension=0, tiled=True),
        lax.psum_scatter(time_acc, ("wide", "narrow"), scatter_dimension=1, tiled=True),
    )
    return (
        out_latents,
        grad_media,
        grad_latents,
        time_sum,
        mg_sum,
        mb_sum,
        lg_sum,
        lb_sum,
        fg_sum,
        fb_sum,
        query_sum,
        keyval_sum,
        output_sum,
        up_sum,
        down_sum,
    )


def solution(mesh):
    placed = (
        P("wide", "narrow", None),
        P("wide", "narrow", None),
        P("wide"),
        P("wide", None),
        P(),
        P(),
        P(),
        P(),
        P(),
        P(),
        P(),
        P("wide", "narrow"),
        P("wide", None, "narrow"),
        P("narrow", "wide"),
        P(None, "narrow"),
        P("narrow", None),
        P("wide", "narrow", None),
    )
    return jax.shard_map(
        body,
        mesh=mesh,
        in_specs=placed,
        out_specs=(
            P("wide", "narrow", None),
            P("wide", "narrow", None),
            P("wide", "narrow", None),
            P(None, ("wide", "narrow")),
            P(("wide", "narrow")),
            P(("wide", "narrow")),
            P(("wide", "narrow")),
            P(("wide", "narrow")),
            P(("wide", "narrow")),
            P(("wide", "narrow")),
            P("wide", "narrow"),
            P("wide", None, "narrow"),
            P("narrow", "wide"),
            P("wide", "narrow"),
            P("narrow", "wide"),
        ),
        check_vma=False,
    )
```

profile of v0, /device:TPU:0, one launch (start us, length us, event | category | flops | bytes accessed | tf_op | source)
XLA Modules:
  0.0 941.4 jit_solution(12498868731809088327)
XLA Ops:
  15.3 6.9 all_gather.36
  23.6 30.5 %all-gather.12.cloned.1.call-done = bf16[1536,384]{1,0:T(8,128)(2,1)} async-done(((bf16[192,384]{1,0:T(8,128)(2,1)}), bf16[1536,384]{1,0:T(8,128)(2,1)}) %all-gather.12.cloned.1.call-update) | async-done | bytes 1179664 | tf_op jit(solution)/shard_map/all_gather | solution.py:77
  55.8 51.6 %all-gather.10.cloned.1.call-done = bf16[1536,2,384]{2,0,1:T(8,128)(2,1)} async-done(((bf16[192,2,384]{2,0,1:T(8,128)(2,1)}), bf16[1536,2,384]{2,0,1:T(8,128)(2,1)}) %all-gather.10.cloned.1.call-update) | async-done | bytes 2359312 | tf_op jit(solution)/shard_map/all_gather | solution.py:78
  107.4 4.3 copy.117
  111.7 42.8 %all-gather.8.cloned.1.call-done = bf16[2048,1536]{1,0:T(8,128)(2,1)} async-done(((bf16[512,1536]{1,0:T(8,128)(2,1)}), bf16[2048,1536]{1,0:T(8,128)(2,1)}) %all-gather.8.cloned.1.call-update) | async-done | bytes 6291472 | tf_op jit(solution)/shard_map/while/body/eval_jaxpr/all_gather | solution.py:115
  157.9 5.5 convolution_convert_fusion.2
  181.3 16.3 %all-gather.14.cloned.1.call-done = bf16[384,1536]{0,1:T(8,128)(2,1)} async-done(((bf16[384,192]{0,1:T(8,128)(2,1)}), bf16[384,1536]{0,1:T(8,128)(2,1)}) %all-gather.14.cloned.1.call-update) | async-done | bytes 1179664 | tf_op jit(solution)/shard_map/all_gather | solution.py:79
  200.1 7.1 all-gather
  207.2 11.8 %reduce-scatter.11.cloned.1.call-done = bf16[16,1536]{1,0:T(8,128)(2,1)} async-done(((bf16[64,1536]{1,0:T(8,128)(2,1)}), bf16[16,1536]{1,0:T(8,128)(2,1)}) %reduce-scatter.11.cloned.1.call-update) | async-done | bytes 49168 | tf_op jit(solution)/shard_map/while/body/eval_jaxpr/reduce_scatter | solution.py:146
  221.9 5.6 all_gather.40
  231.5 4.0 fusion.8
  236.2 4.6 convolution_convert_fusion.7
  241.6 19.1 %reduce-scatter.15.cloned.1.call-done = bf16[16,1536]{1,0:T(8,128)(2,1)} async-done(((bf16[64,1536]{1,0:T(8,128)(2,1)}), bf16[16,1536]{1,0:T(8,128)(2,1)}) %reduce-scatter.15.cloned.1.call-update) | async-done | bytes 49168 | tf_op jit(solution)/shard_map/while/body/eval_jaxpr/reduce_scatter | solution.py:173
  263.2 5.6 all_gather.42
  272.6 22.0 %psum.7 = f32[]{:T(128)} all-reduce(f32[]{:T(128)S(6)} %add.196), channel_id=1, replica_groups=mesh['wide'=8,'narrow'=4] {'wide'}, use_global_device_ids=true, to_apply=%region_14.15 | all-reduce | flops 1 | bytes 8 | tf_op jit(solution)/shard_map/psum | solution.py:73
  295.4 4.2 multiply_reduce_fusion.4
  316.8 10.9 %convolution_convert_fusion.4 = bf16[1536,768]{0,1:T(8,128)(2,1)} fusion(bf16[2112,1536]{1,0:T(8,128)(2,1)} %copy-done.6, bf16[2112,384]{0,1:T(8,128)(2,1)S(1)} %bitcast.160, bf16[2112,384]{0,1:T(8,128)(2,1)S(1)} %bitcast.155), kind=kOutput, calls=%fused_computation.19 | convolution fusion | flops 4990500864 | bytes 12091392 | tf_op jit(solution)/shard_map/while/body/eval_jaxpr/kd,ke->de/dot_general | solution.py:215
  327.7 6.9 copy.135
  338.8 8.7 copy.126
  347.6 4.7 all-to-all-start
  352.3 4.7 convolution_convert_fusion.8
  357.3 31.9 %all-to-all-done = bf16[2048,2,384]{2,1,0:T(2,128)(2,1)} async-done(((bf16[2048,2,384]{2,1,0:T(2,128)(2,1)}), bf16[2048,2,384]{2,1,0:T(2,128)(2,1)}, u32[]{:S(2)}, u32[]{:S(2)}) %all-to-all-start) | async-done | bytes 3145760 | tf_op jit(solution)/shard_map/while/body/eval_jaxpr/all_to_all | solution.py:230
  393.5 10.0 %multiply_reduce_fusion = (f32[1536]{0:T(1024)}, f32[512]{0:T(512)S(1)}, f32[512]{0:T(512)S(1)}, f32[1536]{0:T(1024)}, f32[512,1536]{1,0:T(8,128)S(1)}) fusion(f32[512,1536]{1,0:T(8,128)S(1)} %get-tuple-element.150, f32[512]{0:T(512)S(1)} %add_rsqrt_fusion, f32[512]{0:T(512)S(1)} %broadcast_multiply_fusion.2, f32[1536]{0:T(1024)S(1)} %copy-done.33, ...), kind=kOutput, calls=%fused_computation.23 | convolution fusion | flops 4838912000 | bytes 18900992 | tf_op jit(solution)/shard_map/while/body/eval_jaxpr/rsc,dsc->rd/dot_general | solution.py:233
  413.9 3.9 convolution_convert_fusion
  431.6 31.3 %reduce-scatter.17.cloned.1.call-done = bf16[192,384]{1,0:T(8,128)(2,1)} async-done(((bf16[1536,384]{1,0:T(8,128)(2,1)}), bf16[192,384]{1,0:T(8,128)(2,1)}) %reduce-scatter.17.cloned.1.call-update) | async-done | bytes 147472 | tf_op jit(solution)/shard_map/reduce_scatter | solution.py:306
  464.6 109.4 %all-reduce.11.cloned.1.call-done = bf16[1536,2,384]{2,1,0:T(2,128)(2,1)} async-done(((bf16[1536,2,384]{2,1,0:T(2,128)(2,1)}), bf16[1536,2,384]{2,1,0:T(2,128)(2,1)}) %all-reduce.11.cloned.1.call-update) | async-done | bytes 2359312
  576.0 6.2 convolution_bitcast_fusion.2
  582.3 29.8 %all-gather.18.cloned.1.call-done = bf16[1536,1536]{1,0:T(8,128)(2,1)} async-done(((bf16[1536,384]{1,0:T(8,128)(2,1)}), bf16[1536,1536]{1,0:T(8,128)(2,1)}) %all-gather.18.cloned.1.call-update) | async-done | bytes 4718608 | tf_op jit(solution)/shard_map/all_gather | solution.py:82
  616.0 40.1 %all-reduce.8 = (f32[1536]{0:T(1024)S(1)}, f32[1536]{0:T(1024)S(1)}, f32[1536]{0:T(1024)S(1)}, f32[1536]{0:T(1024)S(1)}, f32[1536]{0:T(1024)S(1)}, /*index=5*/f32[1536]{0:T(1024)S(1)}) all-reduce(f32[1536]{0:T(1024)S(1)} %copy-done.46, f32[1536]{0:T(1024)S(1)} %copy-done.47, ...), channel_id=7, replica_groups=mesh['wide'=8,'narrow'=4] {'wide','narrow'}, use_global_device_ids=true, to_apply=%region_23.24.clone | all-reduce | flops 9216 | bytes 73728
  661.2 74.4 %reduce-scatter.25.cloned.1.call-done = f32[48,8]{1,0:T(8,128)} async-done(((f32[1536,8]{1,0:T(8,128)}), f32[48,8]{1,0:T(8,128)}) %reduce-scatter.25.cloned.1.call-update) | async-done | bytes 1552
  737.0 96.9 %reduce-scatter.21.cloned.1.call-done = bf16[192,1536]{1,0:T(8,128)(2,1)} async-done(((bf16[1536,1536]{1,0:T(8,128)(2,1)}), bf16[192,1536]{1,0:T(8,128)(2,1)}) %reduce-scatter.21.cloned.1.call-update) | async-done | bytes 589840 | tf_op jit(solution)/shard_map/reduce_scatter | solution.py:300
  836.0 96.6 %reduce-scatter.23.cloned.1.call-done = bf16[1536,192]{0,1:T(8,128)(2,1)} async-done(((bf16[1536,1536]{0,1:T(8,128)(2,1)}), bf16[1536,192]{0,1:T(8,128)(2,1)}) %reduce-scatter.23.cloned.1.call-update) | async-done | bytes 589840 | tf_op jit(solution)/shard_map/reduce_scatter | solution.py:303
  (234 shorter events, 115.8 us)
Async XLA Ops:
  7.2 46.9 %all-gather.12.cloned.1.call-start = ((), (), s32[]{:S(2)}) async-start(), calls=%async_computation.12 | async-start | bytes 1327104 | tf_op jit(solution)/shard_map/all_gather | solution.py:77
  7.9 99.4 %all-gather.10.cloned.1.call-start = ((), (), s32[]{:S(2)}) async-start(), calls=%async_computation.11 | async-start | bytes 2654208 | tf_op jit(solution)/shard_map/all_gather | solution.py:78
  9.7 144.7 %all-gather.8.cloned.1.call-start = ((), (), s32[]{:S(2)}) async-start(), calls=%async_computation.10 | async-start | bytes 7864320 | tf_op jit(solution)/shard_map/while/body/eval_jaxpr/all_gather | solution.py:115
  14.2 183.4 %all-gather.14.cloned.1.call-start = ((), (), s32[]{:S(2)}) async-start(), calls=%async_computation.13 | async-start | bytes 1327104 | tf_op jit(solution)/shard_map/all_gather | solution.py:79
  14.8 204.2 %reduce-scatter.11.cloned.1.call-start = ((), (), s32[]{:S(2)}) async-start(), calls=%async_computation.14 | async-start | bytes 245760 | tf_op jit(solution)/shard_map/while/body/eval_jaxpr/reduce_scatter | solution.py:146
  23.5 149.4 %copy-start.54 = (pred[2112]{0:T(1024)(128)(4,1)}, pred[2112]{0:T(1024)(128)(4,1)S(1)}, u32[]{:S(2)}) copy-start(pred[2112]{0:T(1024)(128)(4,1)S(1)} %concatenate.18) | copy-start | bytes 6340
  55.8 117.2 %copy-start.27 = (bf16[64,4,96]{2,1,0:T(4,128)(2,1)}, bf16[64,4,96]{2,1,0:T(4,128)(2,1)S(1)}, u32[]{:S(2)}) copy-start(bf16[64,4,96]{2,1,0:T(4,128)(2,1)S(1)} %reshape.235) | copy-start | bytes 147460
  176.6 127.5 %copy-start.57 = (f32[4,64]{1,0:T(4,128)}, f32[4,64]{1,0:T(4,128)S(1)}, u32[]{:S(2)}) copy-start(f32[4,64]{1,0:T(4,128)S(1)} %get-tuple-element.151) | copy-start | bytes 3076
  176.6 44.4 %copy-start.28 = (f32[1536]{0:T(1024)S(1)}, f32[1536]{0:T(1024)}, u32[]{:S(2)}) copy-start(f32[1536]{0:T(1024)} %param.26) | copy-start | bytes 18436
  176.6 44.4 %copy-start.44 = (f32[1536]{0:T(1024)S(1)}, f32[1536]{0:T(1024)}, u32[]{:S(2)}) copy-start(f32[1536]{0:T(1024)} %param.27) | copy-start | bytes 18436
  181.3 50.1 %copy-start.18 = (f32[64,384]{1,0:T(8,128)}, f32[64,384]{1,0:T(8,128)S(1)}, u32[]{:S(2)}) copy-start(f32[64,384]{1,0:T(8,128)S(1)} %reshape.237) | copy-start | bytes 294916
  200.1 60.6 %reduce-scatter.15.cloned.1.call-start = ((), (), s32[]{:S(2)}) async-start(), calls=%async_computation.16 | async-start | bytes 245760 | tf_op jit(solution)/shard_map/while/body/eval_jaxpr/reduce_scatter | solution.py:173
  220.0 42.3 %copy-start.36 = (f32[16]{0:T(128)}, f32[16]{0:T(128)S(1)}, u32[]{:S(2)}) copy-start(f32[16]{0:T(128)S(1)} %broadcast_multiply_fusion.7) | copy-start | bytes 196
  240.8 54.6 %copy-start.55 = (pred[2112]{0:T(1024)(128)(4,1)S(1)}, pred[2112]{0:T(1024)(128)(4,1)}, u32[]{:S(2)}) copy-start(pred[2112]{0:T(1024)(128)(4,1)} %copy-done.54) | copy-start | bytes 6340
  240.8 152.7 %all-gather.16.cloned.1.call-start = ((), (), s32[]{:S(2)}) async-start(), calls=%async_computation.17 | async-start | bytes 11796480 | tf_op jit(solution)/shard_map/all_gather | solution.py:83
  241.5 188.5 %reduce-scatter.19.cloned.1.call-start = ((), (), s32[]{:S(2)}) async-start(), calls=%async_computation.20 | async-start | bytes 1327104 | tf_op jit(solution)/shard_map/reduce_scatter | solution.py:315
  271.9 191.0 %reduce-scatter.17.cloned.1.call-start = ((), (), s32[]{:S(2)}) async-start(), calls=%async_computation.19 | async-start | bytes 1327104 | tf_op jit(solution)/shard_map/reduce_scatter | solution.py:306
  311.9 262.1 %all-reduce.11.cloned.1.call-start = ((), (), s32[]{:S(2)}) async-start(), calls=%async_computation.24 | async-start | bytes 4718592
  334.6 277.5 %all-gather.18.cloned.1.call-start = ((), (), s32[]{:S(2)}) async-start(), calls=%async_computation.18 | async-start | bytes 5898240 | tf_op jit(solution)/shard_map/all_gather | solution.py:82
  347.6 41.7 %all-to-all-start = ((bf16[2048,2,384]{2,1,0:T(2,128)(2,1)}), bf16[2048,2,384]{2,1,0:T(2,128)(2,1)}, u32[]{:S(2)}, u32[]{:S(2)}) async-start(bf16[2048,2,384]{2,1,0:T(2,128)(2,1)} %copy.126), calls=%async_computation.3 | async-start | bytes 6291456 | tf_op jit(solution)/shard_map/while/body/eval_jaxpr/all_to_all | solution.py:230
  352.3 307.3 %reduce-scatter.13.cloned.1.call-start = ((), (), s32[]{:S(2)}) async-start(), calls=%async_computation.15 | async-start | bytes 245760 | tf_op jit(solution)/shard_map/while/body/eval_jaxpr/reduce_scatter | solution.py:158
  357.0 378.5 %reduce-scatter.25.cloned.1.call-start = ((), (), s32[]{:S(2)}) async-start(), calls=%async_computation.23 | async-start | bytes 811008
  409.3 424.6 %reduce-scatter.21.cloned.1.call-start = ((), (), s32[]{:S(2)}) async-start(), calls=%async_computation.21 | async-start | bytes 5308416 | tf_op jit(solution)/shard_map/reduce_scatter | solution.py:300
  412.9 519.8 %reduce-scatter.23.cloned.1.call-start = ((), (), s32[]{:S(2)}) async-start(), calls=%async_computation.22 | async-start | bytes 5308416 | tf_op jit(solution)/shard_map/reduce_scatter | solution.py:303
  421.3 8.6 all-to-all-start.1
  582.2 77.3 %copy-start.24 = (bf16[16,1536]{1,0:T(8,128)(2,1)S(1)}, bf16[16,1536]{1,0:T(8,128)(2,1)}, u32[]{:S(2)}) copy-start(bf16[16,1536]{1,0:T(8,128)(2,1)} %reduce-scatter.15.cloned.1.call-done) | copy-start | bytes 147460
  582.2 77.3 %copy-start.26 = (bf16[1,16,1536]{2,1,0:T(8,128)(2,1)S(1)}, bf16[1,16,1536]{2,1,0:T(8,128)(2,1)}, u32[]{:S(2)}) copy-start(bf16[1,16,1536]{2,1,0:T(8,128)(2,1)} %param.33) | copy-start | bytes 147460
  582.3 77.3 %copy-start.37 = (f32[16]{0:T(128)S(1)}, f32[16]{0:T(128)}, u32[]{:S(2)}) copy-start(f32[16]{0:T(128)} %copy-done.36) | copy-start | bytes 196
  582.3 77.3 %copy-start.42 = (f32[16]{0:T(128)S(1)}, f32[16]{0:T(128)}, u32[]{:S(2)}) copy-start(f32[16]{0:T(128)} %copy-done.41) | copy-start | bytes 196
  582.3 77.3 %copy-start.51 = (f32[16]{0:T(128)S(1)}, f32[16]{0:T(128)}, u32[]{:S(2)}) copy-start(f32[16]{0:T(128)} %copy-done.50) | copy-start | bytes 196
  582.3 77.3 %copy-start.53 = (f32[16]{0:T(128)S(1)}, f32[16]{0:T(128)}, u32[]{:S(2)}) copy-start(f32[16]{0:T(128)} %copy-done.52) | copy-start | bytes 196
  612.1 322.7 %copy-start.1 = (bf16[8,1536]{1,0:T(8,128)(2,1)S(1)}, bf16[8,1536]{1,0:T(8,128)(2,1)}, u32[]{:S(2)}) copy-start(bf16[8,1536]{1,0:T(8,128)(2,1)} %param.21) | copy-start | bytes 73732
  (44 other events, 471.9 us)
Sparse Core Ops, SparseCore 0:
  10.2 43.8 all-gather.11
  56.8 50.4 all-gather.9
  109.5 44.8 all-gather.7
  156.5 41.1 all-gather.13
  200.5 18.4 reduce-scatter.10
  240.9 19.7 reduce-scatter.14
  262.3 64.0 all-gather.15
  330.4 64.8 reduce-scatter.18
  399.2 63.7 reduce-scatter.16
  466.4 107.5 all-reduce.10
  575.6 36.5 all-gather.17
  614.4 19.8 reduce-scatter.12
  639.4 96.1 reduce-scatter.24
  739.1 94.7 reduce-scatter.20
  837.3 95.2 reduce-scatter.22
where the time goes:
time: 944 us; the launch traced here: 941 us
  waiting for transfers between devices  649 us (69%)
  matrix products  95.8 us (10%)
  blocking collectives  87.2 us (9%)
  local copies, waits for them, and re-layouts  54.7 us (6%)
  other arithmetic  28.2 us (3%)
  between operations  17.4 us (2%)
    unnamed x17, waiting for transfers between devices  187 us
    reduce_scatter x1, waiting for transfers between devices, body(): lax.psum_scatter(up_acc.astype(jnp.bfloat16), 'wide', scatter_dimension=0...  96.9 us
    reduce_scatter x1, waiting for transfers between devices, body(): lax.psum_scatter(down_acc.astype(jnp.bfloat16), 'wide', scatter_dimension...  96.6 us
    all_gather x1, waiting for transfers between devices, body(): lax.all_gather(keyval_weight, 'wide', axis=0, tiled=True)  51.6 us
    all_gather x1, waiting for transfers between devices, item_step(): lax.all_gather(media_nf.astype(jnp.bfloat16), 'narrow', axis=0, tiled=True)  42.8 us
    unnamed x1, blocking collectives  40.1 us
    all_to_all x1, waiting for transfers between devices, item_step(): lax.all_to_all(media_pairs, 'narrow', split_axis=0, concat_axis=2, tiled=...  31.9 us
    reduce_scatter x1, waiting for transfers between devices, body(): lax.psum_scatter(query_acc.astype(jnp.bfloat16), 'wide', scatter_dimensio...  31.3 us
  transfers between devices with their start and end apart: 17, of which 14 were waited for; matrix products, arithmetic and copies ran while one was open for 16% of the time, Pallas kernels for 0%

commit v1 on v0

--- a/solution.py
+++ b/solution.py
@@ -79,7 +79,9 @@
         lax.all_gather(output_weight, "wide", axis=1, tiled=True),
     )
     query_full, keyval_full = (
-        lax.all_gather(query_own, "narrow", axis=1, tiled=True),
+        jnp.concatenate(
+            lax.all_to_all(jnp.stack([query_own] * lax.axis_size("narrow"), 0), "narrow", 0, 0), 1
+        ),
         lax.all_gather(keyval_own, "narrow", axis=2, tiled=True),
     )
     keyval_flat = keyval_own.reshape(width, 2 * cols)

time: 944 us -> 905 us (0.959)
  waiting for transfers between devices: 649 us -> 602 us
    all_gather x1 -> x0, waiting for transfers between devices: 29.8 us -> none  [body(): lax.all_gather(query_own, 'narrow', axis=1, tiled=True)]
    unnamed x17 -> x16, waiting for transfers between devices: 187 us -> 177 us
  transfers between devices with their start and end apart: 17 -> 17, of which waited for: 14 -> 13; matrix products, arithmetic and copies ran while one was open for 16% -> 17% of each run, Pallas kernels for 0% -> 0%
where the time goes in v1:
time: 905 us; the launch traced here: 903 us
  waiting for transfers between devices  602 us (67%)
  matrix products  95.2 us (11%)
  blocking collectives  87.4 us (10%)
  local copies, waits for them, and re-layouts  58 us (6%)
  other arithmetic  28.3 us (3%)
  between operations  17.4 us (2%)
  starting transfers between devices  14.2 us (2%)
    unnamed x16, waiting for transfers between devices  177 us
    reduce_scatter x1, waiting for transfers between devices, body(): lax.psum_scatter(up_acc.astype(jnp.bfloat16), 'wide', scatter_dimension=0...  97 us
    reduce_scatter x1, waiting for transfers between devices, body(): lax.psum_scatter(down_acc.astype(jnp.bfloat16), 'wide', scatter_dimension...  96.6 us
    all_gather x1, waiting for transfers between devices, body(): lax.all_gather(keyval_weight, 'wide', axis=0, tiled=True)  51.6 us
    all_gather x1, waiting for transfers between devices, item_step(): lax.all_gather(media_nf.astype(jnp.bfloat16), 'narrow', axis=0, tiled=True)  42.8 us
    unnamed x1, blocking collectives  40.3 us
    all_to_all x1, waiting for transfers between devices, item_step(): lax.all_to_all(media_pairs, 'narrow', split_axis=0, concat_axis=2, tiled=...  31.9 us
    all_gather x1, waiting for transfers between devices, body(): lax.all_gather(query_weight, 'wide', axis=0, tiled=True)  30.5 us
  transfers between devices with their start and end apart: 17, of which 13 were waited for; matrix products, arithmetic and copies ran while one was open for 17% of the time, Pallas kernels for 0%

profile of v1, /device:TPU:0, one launch (start us, length us, event | category | flops | bytes accessed | tf_op | source)
XLA Modules:
  0.0 902.7 jit_solution(5357242828063476250)
XLA Ops:
  15.3 6.9 all_gather.33
  23.6 30.5 %all-gather.11.cloned.1.call-done = bf16[1536,384]{1,0:T(8,128)(2,1)} async-done(((bf16[192,384]{1,0:T(8,128)(2,1)}), bf16[1536,384]{1,0:T(8,128)(2,1)}) %all-gather.11.cloned.1.call-update) | async-done | bytes 1179664 | tf_op jit(solution)/shard_map/all_gather | solution.py:77
  55.8 51.6 %all-gather.9.cloned.1.call-done = bf16[1536,2,384]{2,0,1:T(8,128)(2,1)} async-done(((bf16[192,2,384]{2,0,1:T(8,128)(2,1)}), bf16[1536,2,384]{2,0,1:T(8,128)(2,1)}) %all-gather.9.cloned.1.call-update) | async-done | bytes 2359312 | tf_op jit(solution)/shard_map/all_gather | solution.py:78
  107.4 4.3 copy.121
  111.7 42.8 %all-gather.7.cloned.1.call-done = bf16[2048,1536]{1,0:T(8,128)(2,1)} async-done(((bf16[512,1536]{1,0:T(8,128)(2,1)}), bf16[2048,1536]{1,0:T(8,128)(2,1)}) %all-gather.7.cloned.1.call-update) | async-done | bytes 6291472 | tf_op jit(solution)/shard_map/while/body/eval_jaxpr/all_gather | solution.py:117
  157.9 5.5 convolution_convert_fusion.2
  181.3 16.3 %all-gather.13.cloned.1.call-done = bf16[384,1536]{0,1:T(8,128)(2,1)} async-done(((bf16[384,192]{0,1:T(8,128)(2,1)}), bf16[384,1536]{0,1:T(8,128)(2,1)}) %all-gather.13.cloned.1.call-update) | async-done | bytes 1179664 | tf_op jit(solution)/shard_map/all_gather | solution.py:79
  200.1 7.1 all-gather
  207.2 11.7 %reduce-scatter.11.cloned.1.call-done = bf16[16,1536]{1,0:T(8,128)(2,1)} async-done(((bf16[64,1536]{1,0:T(8,128)(2,1)}), bf16[16,1536]{1,0:T(8,128)(2,1)}) %reduce-scatter.11.cloned.1.call-update) | async-done | bytes 49168 | tf_op jit(solution)/shard_map/while/body/eval_jaxpr/reduce_scatter | solution.py:148
  221.9 5.6 all_gather.37
  231.5 4.0 fusion.8
  236.2 4.6 convolution_convert_fusion.7
  241.6 19.1 %reduce-scatter.15.cloned.1.call-done = bf16[16,1536]{1,0:T(8,128)(2,1)} async-done(((bf16[64,1536]{1,0:T(8,128)(2,1)}), bf16[16,1536]{1,0:T(8,128)(2,1)}) %reduce-scatter.15.cloned.1.call-update) | async-done | bytes 49168 | tf_op jit(solution)/shard_map/while/body/eval_jaxpr/reduce_scatter | solution.py:175
  263.2 5.6 all_gather.39
  272.6 22.0 %psum.7 = f32[]{:T(128)} all-reduce(f32[]{:T(128)S(6)} %add.196), channel_id=1, replica_groups=mesh['wide'=8,'narrow'=4] {'wide'}, use_global_device_ids=true, to_apply=%region_14.15 | all-reduce | flops 1 | bytes 8 | tf_op jit(solution)/shard_map/psum | solution.py:73
  295.4 4.2 multiply_reduce_fusion.4
  316.8 10.9 %convolution_convert_fusion.4 = bf16[1536,768]{0,1:T(8,128)(2,1)} fusion(bf16[2112,1536]{1,0:T(8,128)(2,1)} %copy-done.6, bf16[2112,384]{0,1:T(8,128)(2,1)S(1)} %bitcast.163, bf16[2112,384]{0,1:T(8,128)(2,1)S(1)} %bitcast.158), kind=kOutput, calls=%fused_computation.19 | convolution fusion | flops 4990500864 | bytes 12091392 | tf_op jit(solution)/shard_map/while/body/eval_jaxpr/kd,ke->de/dot_general | solution.py:217
  327.7 6.9 copy.140
  338.1 8.7 copy.130
  346.9 4.7 all-to-all-start
  351.7 4.7 convolution_convert_fusion.8
  356.7 31.9 %all-to-all-done = bf16[2048,2,384]{2,1,0:T(2,128)(2,1)} async-done(((bf16[2048,2,384]{2,1,0:T(2,128)(2,1)}), bf16[2048,2,384]{2,1,0:T(2,128)(2,1)}, u32[]{:S(2)}, u32[]{:S(2)}) %all-to-all-start) | async-done | bytes 3145760 | tf_op jit(solution)/shard_map/while/body/eval_jaxpr/all_to_all | solution.py:232
  392.9 10.0 %multiply_reduce_fusion = (f32[1536]{0:T(1024)}, f32[512]{0:T(512)S(1)}, f32[512]{0:T(512)S(1)}, f32[1536]{0:T(1024)}, f32[512,1536]{1,0:T(8,128)S(1)}) fusion(f32[512,1536]{1,0:T(8,128)S(1)} %get-tuple-element.150, f32[512]{0:T(512)S(1)} %add_rsqrt_fusion, f32[512]{0:T(512)S(1)} %broadcast_multiply_fusion.2, f32[1536]{0:T(1024)S(1)} %copy-done.34, ...), kind=kOutput, calls=%fused_computation.23 | convolution fusion | flops 4838912000 | bytes 18900992 | tf_op jit(solution)/shard_map/while/body/eval_jaxpr/rsc,dsc->rd/dot_general | solution.py:235
  424.8 4.6 all-to-all-done.1
  432.0 5.4 all-to-all-start.2
  440.3 22.7 %reduce-scatter.17.cloned.1.call-done = bf16[192,384]{1,0:T(8,128)(2,1)} async-done(((bf16[1536,384]{1,0:T(8,128)(2,1)}), bf16[192,384]{1,0:T(8,128)(2,1)}) %reduce-scatter.17.cloned.1.call-update) | async-done | bytes 147472 | tf_op jit(solution)/shard_map/reduce_scatter | solution.py:308
  464.6 109.4 %all-reduce.11.cloned.1.call-done = bf16[1536,2,384]{2,1,0:T(2,128)(2,1)} async-done(((bf16[1536,2,384]{2,1,0:T(2,128)(2,1)}), bf16[1536,2,384]{2,1,0:T(2,128)(2,1)}) %all-reduce.11.cloned.1.call-update) | async-done | bytes 2359312
  576.1 6.2 convolution_bitcast_fusion.2
  585.7 40.3 %all-reduce.8 = (f32[1536]{0:T(1024)S(1)}, f32[1536]{0:T(1024)S(1)}, f32[1536]{0:T(1024)S(1)}, f32[1536]{0:T(1024)S(1)}, f32[1536]{0:T(1024)S(1)}, /*index=5*/f32[1536]{0:T(1024)S(1)}) all-reduce(f32[1536]{0:T(1024)S(1)} %copy-done.47, f32[1536]{0:T(1024)S(1)} %copy-done.48, ...), channel_id=7, replica_groups=mesh['wide'=8,'narrow'=4] {'wide','narrow'}, use_global_device_ids=true, to_apply=%region_23.24.clone | all-reduce | flops 9216 | bytes 73728
  631.1 65.7 %reduce-scatter.25.cloned.1.call-done = f32[48,8]{1,0:T(8,128)} async-done(((f32[1536,8]{1,0:T(8,128)}), f32[48,8]{1,0:T(8,128)}) %reduce-scatter.25.cloned.1.call-update) | async-done | bytes 1552
  698.2 97.0 %reduce-scatter.21.cloned.1.call-done = bf16[192,1536]{1,0:T(8,128)(2,1)} async-done(((bf16[1536,1536]{1,0:T(8,128)(2,1)}), bf16[192,1536]{1,0:T(8,128)(2,1)}) %reduce-scatter.21.cloned.1.call-update) | async-done | bytes 589840 | tf_op jit(solution)/shard_map/reduce_scatter | solution.py:302
  797.4 96.6 %reduce-scatter.23.cloned.1.call-done = bf16[1536,192]{0,1:T(8,128)(2,1)} async-done(((bf16[1536,1536]{0,1:T(8,128)(2,1)}), bf16[1536,192]{0,1:T(8,128)(2,1)}) %reduce-scatter.23.cloned.1.call-update) | async-done | bytes 589840 | tf_op jit(solution)/shard_map/reduce_scatter | solution.py:305
  (237 shorter events, 117.8 us)
Async XLA Ops:
  7.2 46.9 %all-gather.11.cloned.1.call-start = ((), (), s32[]{:S(2)}) async-start(), calls=%async_computation.13 | async-start | bytes 1327104 | tf_op jit(solution)/shard_map/all_gather | solution.py:77
  7.9 99.4 %all-gather.9.cloned.1.call-start = ((), (), s32[]{:S(2)}) async-start(), calls=%async_computation.12 | async-start | bytes 2654208 | tf_op jit(solution)/shard_map/all_gather | solution.py:78
  9.7 144.7 %all-gather.7.cloned.1.call-start = ((), (), s32[]{:S(2)}) async-start(), calls=%async_computation.11 | async-start | bytes 7864320 | tf_op jit(solution)/shard_map/while/body/eval_jaxpr/all_gather | solution.py:117
  14.2 183.4 %all-gather.13.cloned.1.call-start = ((), (), s32[]{:S(2)}) async-start(), calls=%async_computation.14 | async-start | bytes 1327104 | tf_op jit(solution)/shard_map/all_gather | solution.py:79
  14.8 204.2 %reduce-scatter.11.cloned.1.call-start = ((), (), s32[]{:S(2)}) async-start(), calls=%async_computation.15 | async-start | bytes 245760 | tf_op jit(solution)/shard_map/while/body/eval_jaxpr/reduce_scatter | solution.py:148
  23.5 149.4 %copy-start.55 = (pred[2112]{0:T(1024)(128)(4,1)}, pred[2112]{0:T(1024)(128)(4,1)S(1)}, u32[]{:S(2)}) copy-start(pred[2112]{0:T(1024)(128)(4,1)S(1)} %concatenate.18) | copy-start | bytes 6340
  55.8 117.2 %copy-start.28 = (bf16[64,4,96]{2,1,0:T(4,128)(2,1)}, bf16[64,4,96]{2,1,0:T(4,128)(2,1)S(1)}, u32[]{:S(2)}) copy-start(bf16[64,4,96]{2,1,0:T(4,128)(2,1)S(1)} %reshape.243) | copy-start | bytes 147460
  176.6 127.5 %copy-start.58 = (f32[4,64]{1,0:T(4,128)}, f32[4,64]{1,0:T(4,128)S(1)}, u32[]{:S(2)}) copy-start(f32[4,64]{1,0:T(4,128)S(1)} %get-tuple-element.151) | copy-start | bytes 3076
  176.6 44.4 %copy-start.29 = (f32[1536]{0:T(1024)S(1)}, f32[1536]{0:T(1024)}, u32[]{:S(2)}) copy-start(f32[1536]{0:T(1024)} %param.26) | copy-start | bytes 18436
  176.6 44.4 %copy-start.45 = (f32[1536]{0:T(1024)S(1)}, f32[1536]{0:T(1024)}, u32[]{:S(2)}) copy-start(f32[1536]{0:T(1024)} %param.27) | copy-start | bytes 18436
  181.3 50.1 %copy-start.19 = (f32[64,384]{1,0:T(8,128)}, f32[64,384]{1,0:T(8,128)S(1)}, u32[]{:S(2)}) copy-start(f32[64,384]{1,0:T(8,128)S(1)} %reshape.245) | copy-start | bytes 294916
  200.1 60.6 %reduce-scatter.15.cloned.1.call-start = ((), (), s32[]{:S(2)}) async-start(), calls=%async_computation.17 | async-start | bytes 245760 | tf_op jit(solution)/shard_map/while/body/eval_jaxpr/reduce_scatter | solution.py:175
  220.0 42.3 %copy-start.37 = (f32[16]{0:T(128)}, f32[16]{0:T(128)S(1)}, u32[]{:S(2)}) copy-start(f32[16]{0:T(128)S(1)} %broadcast_multiply_fusion.7) | copy-start | bytes 196
  240.7 54.6 %copy-start.56 = (pred[2112]{0:T(1024)(128)(4,1)S(1)}, pred[2112]{0:T(1024)(128)(4,1)}, u32[]{:S(2)}) copy-start(pred[2112]{0:T(1024)(128)(4,1)} %copy-done.55) | copy-start | bytes 6340
  240.8 152.2 %all-gather.15.cloned.1.call-start = ((), (), s32[]{:S(2)}) async-start(), calls=%async_computation.18 | async-start | bytes 11796480 | tf_op jit(solution)/shard_map/all_gather | solution.py:85
  241.5 197.2 %reduce-scatter.19.cloned.1.call-start = ((), (), s32[]{:S(2)}) async-start(), calls=%async_computation.20 | async-start | bytes 1327104 | tf_op jit(solution)/shard_map/reduce_scatter | solution.py:317
  271.9 191.1 %reduce-scatter.17.cloned.1.call-start = ((), (), s32[]{:S(2)}) async-start(), calls=%async_computation.19 | async-start | bytes 1327104 | tf_op jit(solution)/shard_map/reduce_scatter | solution.py:308
  311.9 262.2 %all-reduce.11.cloned.1.call-start = ((), (), s32[]{:S(2)}) async-start(), calls=%async_computation.24 | async-start | bytes 4718592
  346.9 41.7 %all-to-all-start = ((bf16[2048,2,384]{2,1,0:T(2,128)(2,1)}), bf16[2048,2,384]{2,1,0:T(2,128)(2,1)}, u32[]{:S(2)}, u32[]{:S(2)}) async-start(bf16[2048,2,384]{2,1,0:T(2,128)(2,1)} %copy.130), calls=%async_computation.3 | async-start | bytes 6291456 | tf_op jit(solution)/shard_map/while/body/eval_jaxpr/all_to_all | solution.py:232
  351.7 277.9 %reduce-scatter.13.cloned.1.call-start = ((), (), s32[]{:S(2)}) async-start(), calls=%async_computation.16 | async-start | bytes 245760 | tf_op jit(solution)/shard_map/while/body/eval_jaxpr/reduce_scatter | solution.py:160
  356.4 340.4 %reduce-scatter.25.cloned.1.call-start = ((), (), s32[]{:S(2)}) async-start(), calls=%async_computation.23 | async-start | bytes 811008
  408.7 386.5 %reduce-scatter.21.cloned.1.call-start = ((), (), s32[]{:S(2)}) async-start(), calls=%async_computation.21 | async-start | bytes 5308416 | tf_op jit(solution)/shard_map/reduce_scatter | solution.py:302
  412.4 481.6 %reduce-scatter.23.cloned.1.call-start = ((), (), s32[]{:S(2)}) async-start(), calls=%async_computation.22 | async-start | bytes 5308416 | tf_op jit(solution)/shard_map/reduce_scatter | solution.py:305
  420.8 8.6 all-to-all-start.1
  432.0 150.4 %all-to-all-start.2 = ((bf16[4,1536,384]{1,2,0:T(8,128)(2,1)}), bf16[4,1536,384]{1,2,0:T(8,128)(2,1)}, u32[]{:S(2)}, u32[]{:S(2)}) async-start(bf16[4,1536,384]{1,2,0:T(8,128)(2,1)} %stack.2), calls=%async_computation.5 | async-start | bytes 9437184 | tf_op jit(solution)/shard_map/all_to_all | solution.py:83
  582.3 47.2 %copy-start.25 = (bf16[16,1536]{1,0:T(8,128)(2,1)S(1)}, bf16[16,1536]{1,0:T(8,128)(2,1)}, u32[]{:S(2)}) copy-start(bf16[16,1536]{1,0:T(8,128)(2,1)} %reduce-scatter.15.cloned.1.call-done) | copy-start | bytes 147460
  582.3 47.2 %copy-start.27 = (bf16[1,16,1536]{2,1,0:T(8,128)(2,1)S(1)}, bf16[1,16,1536]{2,1,0:T(8,128)(2,1)}, u32[]{:S(2)}) copy-start(bf16[1,16,1536]{2,1,0:T(8,128)(2,1)} %param.33) | copy-start | bytes 147460
  582.4 47.2 %copy-start.38 = (f32[16]{0:T(128)S(1)}, f32[16]{0:T(128)}, u32[]{:S(2)}) copy-start(f32[16]{0:T(128)} %copy-done.37) | copy-start | bytes 196
  582.4 47.2 %copy-start.43 = (f32[16]{0:T(128)S(1)}, f32[16]{0:T(128)}, u32[]{:S(2)}) copy-start(f32[16]{0:T(128)} %copy-done.42) | copy-start | bytes 196
  582.4 47.2 %copy-start.52 = (f32[16]{0:T(128)S(1)}, f32[16]{0:T(128)}, u32[]{:S(2)}) copy-start(f32[16]{0:T(128)} %copy-done.51) | copy-start | bytes 196
  582.4 47.2 %copy-start.54 = (f32[16]{0:T(128)S(1)}, f32[16]{0:T(128)}, u32[]{:S(2)}) copy-start(f32[16]{0:T(128)} %copy-done.53) | copy-start | bytes 196
  582.4 313.8 %copy-start.1 = (bf16[8,1536]{1,0:T(8,128)(2,1)S(1)}, bf16[8,1536]{1,0:T(8,128)(2,1)}, u32[]{:S(2)}) copy-start(bf16[8,1536]{1,0:T(8,128)(2,1)} %param.21) | copy-start | bytes 73732
  (45 other events, 326.3 us)
Sparse Core Ops, SparseCore 0:
  10.2 43.8 all-gather.10
  56.8 50.4 all-gather.8
  109.5 44.8 all-gather.6
  156.5 41.1 all-gather.12
  200.5 18.4 reduce-scatter.10
  240.9 19.7 reduce-scatter.14
  262.3 64.0 all-gather.14
  330.3 64.8 reduce-scatter.18
  399.2 63.7 reduce-scatter.16
  466.4 107.6 all-reduce.10
  576.5 19.1 reduce-scatter.12
  600.7 95.9 reduce-scatter.24
  700.4 94.6 reduce-scatter.20
  798.7 95.2 reduce-scatter.22
